TPU v7x, 256 devices: a whole 4x4x8 slice. The times are simulated.
256 devices in a mesh: depth: 8 (over x_lo, y), row: 32 (over x_hi, z, core).
Axes of the slice: x: 4 (x_hi: 2, x_lo: 2; x = x_hi * 2 + x_lo), y: 4, z: 8, core: 2. Of those that a mesh axis runs over, the one named last changes fastest.
Arguments:
- field: float32 [2, 8, 4096, 4096], P(None, 'depth', 'row'), may hold values from -6 to 6
- hologram: float32 [4096, 4096], P('row'), may hold values from -16 to 16
- defocus: float32 [8], P('depth'), may hold values from 512 to 2048
Outputs:
- estimate: float32 [2, 8, 4096, 4096], P(None, 'depth', 'row')
All inputs are finite; a program needn't handle non-finite values.
Results may differ from a plain program's by a relative error of at most 0.00045.
Values sent between devices are 32-bit elements; how exact they have to be, the bound alone decides.
A program may use at most 320 MiB of HBM per device.

v0:
```python
import math
import jax
import jax.numpy as jnp
from jax import lax
from jax.sharding import PartitionSpec as P

tv_step_size = 1.0 / 12.0
tv_sharpness = 0.25


def passed_along(block, axis, distance):
    devices = range(lax.axis_size(axis))
    route = [(i - distance, i) for i in devices if i - distance in devices]
    return lax.ppermute(block, axis, route)


def split_length(length_total):
    smaller = 1
    candidate = 1
    while candidate * candidate <= length_total:
        if length_total % candidate == 0:
            smaller = candidate
        candidate = candidate + 1
    return (smaller, length_total // smaller)


def block_table(cosines, sines):
    return jnp.stack([jnp.stack([cosines, -sines]), jnp.stack([sines, cosines])])


def dft_tables(length_total, inverse):
    outer_len, inner_len = split_length(length_total)
    direction = 2.0 * math.pi if inverse else -2.0 * math.pi
    first_k = jnp.arange(outer_len, dtype=jnp.int32)[:, None]
    first_a = jnp.arange(outer_len, dtype=jnp.int32)[None, :]
    radians_one = (first_k * first_a % outer_len).astype(jnp.float32) * (direction / outer_len)
    first_table = block_table(jnp.cos(radians_one), jnp.sin(radians_one))
    second_k = jnp.arange(outer_len, dtype=jnp.int32)[:, None, None]
    second_b = jnp.arange(inner_len, dtype=jnp.int32)[None, :, None]
    second_m = jnp.arange(inner_len, dtype=jnp.int32)[None, None, :]
    whole_index = (second_k * second_b + second_b * second_m * outer_len) % length_total
    radians_two = whole_index.astype(jnp.float32) * (direction / length_total)
    scale = 1.0 / length_total if inverse else 1.0
    second_table = block_table(jnp.cos(radians_two) * scale, jnp.sin(radians_two) * scale)
    return (first_table, second_table, outer_len, inner_len)


def contract(formula, table, data):
    return jnp.einsum(
        formula, table, data, precision=lax.Precision.HIGHEST, preferred_element_type=jnp.float32
    )


def transform_last(data, tables, real_input, real_only):
    first_table, second_table, outer_len, inner_len = tables
    if real_input:
        data = data[None]
        first_table = first_table[:, :1]
    if real_only:
        second_table = second_table[:1]
    leading = data.shape[1:-1]
    folded = data.reshape((data.shape[0],) + leading + (outer_len, inner_len))
    middle = contract("rqka,q...ab->r...kb", first_table, folded)
    result = contract("rqkbm,q...kb->r...mk", second_table, middle)
    result = result.reshape((result.shape[0],) + leading + (outer_len * inner_len,))
    if real_only:
        return result[0]
    return result


def transform_rows(data, tables):
    first_table, second_table, outer_len, inner_len = tables
    leading = data.shape[1:-2]
    trailing = data.shape[-1]
    folded = data.reshape((2,) + leading + (outer_len, inner_len, trailing))
    middle = contract("rqka,q...abc->r...kbc", first_table, folded)
    result = contract("rqkbm,q...kbc->r...mkc", second_table, middle)
    return result.reshape((2,) + leading + (outer_len * inner_len, trailing))


def centred_squares(length_total, offset_start, length_part):
    indices = offset_start + jnp.arange(length_part, dtype=jnp.int32)
    centred = jnp.where(indices < length_total // 2, indices, indices - length_total)
    return (centred * centred).astype(jnp.float32)


def transfer_phase(depth_values, length_total, column_start, column_len):
    ky_squares = centred_squares(length_total, 0, length_total)
    kx_squares = centred_squares(length_total, column_start, column_len)
    grid_sum = (ky_squares[:, None] + kx_squares[None, :]) * (
        math.pi / (length_total * length_total)
    )
    return depth_values[:, None, None] * grid_sum[None]


def ahead_diff(values, incoming, axis_pos):
    extent = values.shape[axis_pos]
    shifted = jnp.concatenate(
        [lax.slice_in_dim(values, 1, extent, axis=axis_pos), incoming], axis=axis_pos
    )
    return shifted - values


def behind_diff(values, incoming, axis_pos):
    extent = values.shape[axis_pos]
    shifted = jnp.concatenate(
        [incoming, lax.slice_in_dim(values, 0, extent - 1, axis=axis_pos)], axis=axis_pos
    )
    return values - shifted


def flux_terms(depth_diff, row_diff, col_diff):
    magnitude = jnp.sqrt(
        jnp.sum(depth_diff * depth_diff + row_diff * row_diff + col_diff * col_diff, axis=0)
    )
    factor = 1.0 / (1.0 + tv_sharpness * magnitude)
    return (depth_diff * factor, row_diff * factor, col_diff * factor)


def shrink_shifts(moved_field, depth_index, row_index, plane_total, length_total):
    planes_dev = moved_field.shape[1]
    rows_dev = moved_field.shape[2]
    plane_next = passed_along(moved_field, "depth", -1)
    row_next = passed_along(moved_field[:, :, :1], "row", -1)
    plane_ids = depth_index * planes_dev + jnp.arange(planes_dev, dtype=jnp.int32)
    row_ids = row_index * rows_dev + jnp.arange(rows_dev, dtype=jnp.int32)
    depth_diff = jnp.where(
        (plane_ids == plane_total - 1)[None, :, None, None],
        0.0,
        ahead_diff(moved_field, plane_next, 1),
    )
    row_diff = jnp.where(
        (row_ids == length_total - 1)[None, None, :, None],
        0.0,
        ahead_diff(moved_field, row_next, 2),
    )
    col_diff = ahead_diff(moved_field, moved_field[..., -1:], 3)
    flux_z, flux_y, flux_x = flux_terms(depth_diff, row_diff, col_diff)
    prior_plane = passed_along(flux_z, "depth", 1)
    prior_row = passed_along(flux_y[:, :, -1:], "row", 1)
    divergence = (
        behind_diff(flux_z, prior_plane, 1)
        + behind_diff(flux_y, prior_row, 2)
        + behind_diff(flux_x, jnp.zeros_like(flux_x[..., :1]), 3)
    )
    return moved_field + tv_step_size * divergence


def per_device(field, hologram, defocus):
    planes_dev = field.shape[1]
    rows_dev = field.shape[2]
    length_total = field.shape[3]
    row_devices = lax.axis_size("row")
    depth_devices = lax.axis_size("depth")
    row_index = lax.axis_index("row")
    depth_index = lax.axis_index("depth")
    cols_dev = length_total // row_devices
    rows_piece = rows_dev // depth_devices
    plane_total = planes_dev * depth_devices
    forward_tables = dft_tables(length_total, False)
    inverse_tables = dft_tables(length_total, True)
    phase_table = transfer_phase(defocus, length_total, row_index * cols_dev, cols_dev)
    cosine_table = jnp.cos(phase_table)
    sine_table = jnp.sin(phase_table)
    hologram_part = lax.dynamic_slice_in_dim(hologram, depth_index * rows_piece, rows_piece, 0)
    estimate = field
    spectrum = transform_last(estimate, forward_tables, False, False)
    spectrum = lax.all_to_all(spectrum, "row", split_axis=3, concat_axis=2, tiled=True)
    spectrum = transform_rows(spectrum, forward_tables)
    sum_real = jnp.sum(spectrum[0] * cosine_table + spectrum[1] * sine_table, axis=0)
    sum_imag = jnp.sum(spectrum[1] * cosine_table - spectrum[0] * sine_table, axis=0)
    summed = transform_rows(jnp.stack([sum_real, sum_imag]), inverse_tables)
    by_rows = lax.all_to_all(summed, "row", split_axis=1, concat_axis=2, tiled=True)
    image_part = transform_last(by_rows, inverse_tables, False, True)
    image_sum = lax.psum_scatter(image_part, "depth", scatter_dimension=0, tiled=True)
    misfit = image_sum - hologram_part
    misfit_block = lax.all_gather(misfit, "depth", axis=0, tiled=True)
    misfit_pair = transform_last(misfit_block, forward_tables, True, False)
    misfit_spec = lax.all_to_all(misfit_pair, "row", split_axis=2, concat_axis=1, tiled=True)
    misfit_spec = transform_rows(misfit_spec, forward_tables)
    adj_real = misfit_spec[0][None] * cosine_table - misfit_spec[1][None] * sine_table
    adj_imag = misfit_spec[0][None] * sine_table + misfit_spec[1][None] * cosine_table
    adjoint = transform_rows(jnp.stack([adj_real, adj_imag]), inverse_tables)
    adjoint = lax.all_to_all(adjoint, "row", split_axis=2, concat_axis=3, tiled=True)
    gradient = transform_last(adjoint, inverse_tables, False, False)
    moved_field = estimate - 1.0 / plane_total * gradient
    estimate = shrink_shifts(moved_field, depth_index, row_index, plane_total, length_total)
    return estimate


def solution(mesh):
    return jax.shard_map(
        per_device,
        mesh=mesh,
        in_specs=(P(None, "depth", "row", None), P("row", None), P("depth")),
        out_specs=P(None, "depth", "row", None),
        check_vma=False,
    )
```

profile of v0, /device:TPU:34, one launch (start us, length us, event | category | flops | bytes accessed | tf_op | source)
XLA Modules:
  0.0 1049.4 jit_solution(16027976916007795739)
XLA Ops:
  12.7 17.3 %fusion.100 = (f32[1,64,64,64]{2,3,0,1:T(8,128)S(1)}, f32[1,64,64,64]{2,3,0,1:T(8,128)}, f32[1,64,64,64]{2,3,0,1:T(8,128)}, f32[1,64,64,64]{2,3,0,1:T(8,128)}, f...) fusion(s32[64,64]{0,1:T(8,128)S(1)} %broadcast_multiply_fusion.3, s32[64,64]{1,0:T(8,128)S(1)} %copy.91), kind=kLoop, calls=%fused_computation.103 | loop fusion | flops 4980736 | bytes 6324224 | tf_op jit(solution)/shard_map/neg | solution.py:28
  38.1 11.0 %fusion.46 = f32[2,1,128,64,64]{2,3,0,4,1:T(8,128)S(1)} fusion(f32[1,2,64,64,64]{3,4,1,0,2:T(8,128)S(1)} %get-tuple-element.13, f32[1,2,64,64,64]{3,4,1,0,2:T(8,128)S(1)} %get-tuple-element.12, f32[2,128,64,64,1]{1,2,3,0,4:T(8,128)S(1)} %fusion.43), kind=kOutput, calls=%fused_computation.64 | convolution fusion | flops 1611661312 | bytes 12582912 | tf_op jit(solution)/shard_map/rqkbm,q...kb->r...mk/dot_general | solution.py:49
  51.6 16.2 %copy.95 = f32[2,1,128,4096]{2,0,1,3:T(2,128)} copy(f32[2,1,128,4096]{2,3,0,1:T(8,128)S(1)} %bitcast.244) | data formatting | bytes 8388608 | tf_op jit(solution)/shard_map/reshape | solution.py:65
  67.8 10.3 all-to-all-start
  79.2 8.7 fusion.42
  87.9 85.5 %all-to-all-done = f32[2,1,128,4096]{2,0,1,3:T(2,128)} async-done(((f32[2,1,128,4096]{2,0,1,3:T(2,128)}), f32[2,1,128,4096]{2,0,1,3:T(2,128)}, u32[]{:S(2)}, u32[]{:S(2)}) %all-to-all-start) | async-done | bytes 4194336 | tf_op jit(solution)/shard_map/all_to_all | solution.py:168
  183.5 8.8 fusion.49
  192.4 10.0 fusion.52
  202.4 8.3 multiply_add_fusion.1
  214.6 10.4 fusion.76
  227.4 15.6 %copy.105 = f32[2,4096,128]{2,0,1:T(2,128)S(1)} copy(f32[2,4096,128]{2,1,0:T(8,128)S(1)} %bitcast.247) | data formatting | bytes 8388608 | tf_op jit(solution)/shard_map/reshape | solution.py:78
  243.1 105.9 %all_to_all.60 = f32[2,4096,128]{2,0,1:T(2,128)S(1)} all-to-all(f32[2,4096,128]{2,0,1:T(2,128)S(1)} %copy.105), channel_id=1, replica_groups=mesh['depth'=8,'row'=32] {'row'}, dimensions={1} | all-to-all | bytes 8388608 | tf_op jit(solution)/shard_map/all_to_all | solution.py:173
  356.9 8.8 fusion.58
  365.7 6.5 fusion.97
  378.4 39.3 %reduce-scatter.4.cloned.1.call-done = f32[16,4096]{1,0:T(8,128)} async-done(((f32[128,4096]{1,0:T(8,128)}), f32[16,4096]{1,0:T(8,128)}) %reduce-scatter.4.cloned.1.call-update) | async-done | bytes 262160
  426.7 43.0 %all-gather.2.cloned.1.call-done = f32[128,4096]{1,0:T(8,128)} async-done(((f32[16,4096]{1,0:T(8,128)}), f32[128,4096]{1,0:T(8,128)}) %all-gather.2.cloned.1.call-update) | async-done | bytes 2097168 | tf_op jit(solution)/shard_map/all_gather | solution.py:177
  476.6 12.6 %fusion.61 = f32[2,128,64,64]{1,2,0,3:T(8,128)S(1)} fusion(f32[1,2,64,64,64]{3,4,1,0,2:T(8,128)} %copy-done.6, f32[1,2,64,64,64]{3,4,1,0,2:T(8,128)S(1)} %copy-done.4, f32[2,128,64,64,1]{1,2,0,3,4:T(8,128)S(1)} %convolution_bitcast_fusion), kind=kOutput, calls=%fused_computation.69 | convolution fusion | flops 1611661312 | bytes 12582912 | tf_op jit(solution)/shard_map/rqkbm,q...kb->r...mk/dot_general | solution.py:49
  491.7 15.6 %copy.117 = f32[2,128,4096]{1,0,2:T(2,128)S(1)} copy(f32[2,128,4096]{1,2,0:T(8,128)S(1)} %bitcast.250) | data formatting | bytes 8388608 | tf_op jit(solution)/shard_map/reshape | solution.py:65
  507.3 107.2 %all_to_all.61 = f32[2,128,4096]{1,0,2:T(2,128)S(1)} all-to-all(f32[2,128,4096]{1,0,2:T(2,128)S(1)} %copy.117), channel_id=1, replica_groups=mesh['depth'=8,'row'=32] {'row'}, dimensions={2} | all-to-all | bytes 8388608 | tf_op jit(solution)/shard_map/all_to_all | solution.py:179
  622.4 8.7 fusion.64
  631.1 10.0 fusion.67
  641.1 8.3 multiply_subtract_fusion
  653.5 10.4 fusion.81
  666.3 15.6 %copy.127 = f32[2,1,4096,128]{3,0,1,2:T(2,128)S(1)} copy(f32[2,1,4096,128]{3,2,0,1:T(8,128)S(1)} %bitcast.252) | data formatting | bytes 8388608 | tf_op jit(solution)/shard_map/reshape | solution.py:78
  682.0 101.2 %all_to_all.62 = f32[2,1,4096,128]{3,0,1,2:T(2,128)S(1)} all-to-all(f32[2,1,4096,128]{3,0,1,2:T(2,128)S(1)} %copy.127), channel_id=1, replica_groups=mesh['depth'=8,'row'=32] {'row'}, dimensions={2} | all-to-all | bytes 8388608 | tf_op jit(solution)/shard_map/all_to_all | solution.py:184
  791.1 8.8 fusion.73
  799.9 10.0 fusion.11
  836.9 71.8 %collective-permute-done = f32[2,1,128,4096]{2,3,0,1:T(8,128)} collective-permute-done((f32[2,1,128,4096]{2,3,0,1:T(8,128)}, f32[2,1,128,4096]{2,3,0,1:T(8,128)}, u32[]{:S(2)}, u32[]{:S(2)}) %collective-permute-start) | collective-permute-done | bytes 4194336 | tf_op jit(solution)/shard_map/ppermute | solution.py:14
  908.7 9.1 add_reduce_fusion
  920.1 7.2 broadcast_multiply_fusion.2
  943.2 79.4 %collective-permute-done.2 = f32[2,1,128,4096]{2,3,0,1:T(8,128)} collective-permute-done((f32[2,1,128,4096]{2,3,0,1:T(8,128)}, f32[2,1,128,4096]{2,3,0,1:T(8,128)}, u32[]{:S(2)}, u32[]{:S(2)}) %collective-permute-start.2) | collective-permute-done | bytes 4194336 | tf_op jit(solution)/shard_map/ppermute | solution.py:14
  1022.6 14.0 %fusion.10 = f32[2,1,128,4096]{2,3,0,1:T(8,128)} fusion(f32[2,1,128,4096]{2,3,0,1:T(8,128)} %bitcast_subtract_fusion, f32[2,1,128,4096]{2,3,0,1:T(8,128)} %copy-done.9, f32[2,1,127,4096]{2,3,0,1:T(8,128)} %bitcast.239, f32[2,1,1,4096]{2,3,0,1:T(8,128)} %copy.138, f32[2,1,128,4096]{2,3,0,1:T(8,128)} %get-tuple-element.7, f32[2,1,128,4095]{2,3,0,1:T(8,128)} %bitcast.240, ...), kind=kLoop, calls=%fused_computation.21 | loop fusion | flops 8388608 | bytes 33553408 | tf_op jit(solution)/shard_map/add | solution.py:146
  (106 shorter events, 138.9 us)
Async XLA Ops:
  6.5 371.2 %copy-start = (f32[128,4096]{1,0:T(8,128)S(1)}, f32[128,4096]{1,0:T(8,128)}, u32[]{:S(2)}) copy-start(f32[128,4096]{1,0:T(8,128)} %param.4) | copy-start | bytes 6291460
  30.0 2.2 copy-start.16
  31.7 6.4 copy-start.2
  31.7 6.4 copy-start.6
  67.8 105.6 %all-to-all-start = ((f32[2,1,128,4096]{2,0,1,3:T(2,128)}), f32[2,1,128,4096]{2,0,1,3:T(2,128)}, u32[]{:S(2)}, u32[]{:S(2)}) async-start(f32[2,1,128,4096]{2,0,1,3:T(2,128)} %copy.95), calls=%async_computation | async-start | bytes 8388608 | tf_op jit(solution)/shard_map/all_to_all | solution.py:168
  78.2 339.5 %reduce-scatter.4.cloned.1.call-start = ((), (), s32[]{:S(2)}) async-start(), calls=%async_computation.6 | async-start | bytes 2359296
  183.5 8.8 copy-start.3
  183.5 8.8 copy-start.7
  210.6 3.9 copy-start.10
  210.7 3.9 copy-start.13
  356.9 8.8 copy-start.21
  356.9 8.8 copy-start.22
  377.7 92.0 %all-gather.2.cloned.1.call-start = ((), (), s32[]{:S(2)}) async-start(), calls=%async_computation.5 | async-start | bytes 2359296 | tf_op jit(solution)/shard_map/all_gather | solution.py:177
  471.9 4.8 copy-start.4
  622.4 8.7 copy-start.5
  622.4 8.7 copy-start.8
  649.4 4.1 copy-start.11
  649.4 4.1 copy-start.14
  791.0 8.8 copy-start.12
  791.0 8.8 copy-start.15
  809.9 2.7 copy-start.17
  815.0 93.8 %collective-permute-start = (f32[2,1,128,4096]{2,3,0,1:T(8,128)}, f32[2,1,128,4096]{2,3,0,1:T(8,128)}, u32[]{:S(2)}, u32[]{:S(2)}) collective-permute-start(f32[2,1,128,4096]{2,3,0,1:T(8,128)} %bitcast_subtract_fusion), channel_id=1, source_target_pairs={{32,0},{64,32},{96,64},{128,96},{160,128},{192,160},{224,192},{33,... | collective-permute-start | bytes 12582920 | tf_op jit(solution)/shard_map/ppermute | solution.py:14
  821.8 12.5 %collective-permute-start.1 = (f32[2,1,1,4096]{3,0,2,1:T(2,128)S(1)}, f32[2,1,1,4096]{3,0,2,1:T(2,128)S(1)}, u32[]{:S(2)}, u32[]{:S(2)}) collective-permute-start(f32[2,1,1,4096]{3,0,2,1:T(2,128)S(1)} %copy.135), channel_id=1, source_target_pairs={{1,0},{2,1},{3,2},{4,3},{5,4},{6,5},{7,6},{8,7},{9,8},{10,9},{11,1... | collective-permute-start | bytes 98312 | tf_op jit(solution)/shard_map/ppermute | solution.py:14
  908.7 9.9 copy-start.19
  908.7 9.9 copy-start.20
  917.8 2.3 copy-start.18
  927.3 2.0 copy-start.9
  927.3 95.3 %collective-permute-start.2 = (f32[2,1,128,4096]{2,3,0,1:T(8,128)}, f32[2,1,128,4096]{2,3,0,1:T(8,128)}, u32[]{:S(2)}, u32[]{:S(2)}) collective-permute-start(f32[2,1,128,4096]{2,3,0,1:T(8,128)} %get-tuple-element.5), channel_id=1, source_target_pairs={{0,32},{32,64},{64,96},{96,128},{128,160},{160,192},{192,224},{1,3... | collective-permute-start | bytes 12582920 | tf_op jit(solution)/shard_map/ppermute | solution.py:14
  935.3 5.2 collective-permute-start.3
  1022.6 19.6 %copy-start.1 = (f32[128,4096]{1,0:T(8,128)S(1)}, f32[128,4096]{1,0:T(8,128)}, u32[]{:S(2)}) copy-start(f32[128,4096]{1,0:T(8,128)} %param.4) | copy-start | bytes 6291460
Sparse Core Ops, SparseCore 0:
  377.8 39.8 reduce-scatter.3
  426.8 42.8 all-gather.1
where the time goes:
time: 1060 us; the launch traced here: 1050 us
  waiting for transfers between devices  322 us (30%)
  blocking collectives  314 us (30%)
  local copies, waits for them, and re-layouts  162 us (15%)
  matrix products  134 us (13%)
  other arithmetic  81.5 us (8%)
  starting transfers between devices  20.1 us (2%)
  between operations  15 us (1%)
    ppermute x4, waiting for transfers between devices, passed_along(): return lax.ppermute(block, axis, route)  155 us
    dot_general x16, matrix products, contract(): jnp.einsum(formula, table, data, precision=lax.Precision.HIGHEST, preferr...  134 us
    all_to_all x1, blocking collectives, per_device(): lax.all_to_all(misfit_pair, 'row', split_axis=2, concat_axis=1, tiled=True)  107 us
    all_to_all x1, blocking collectives, per_device(): lax.all_to_all(summed, 'row', split_axis=1, concat_axis=2, tiled=True)  106 us
    all_to_all x1, blocking collectives, per_device(): lax.all_to_all(adjoint, 'row', split_axis=2, concat_axis=3, tiled=True)  101 us
    all_to_all x1, waiting for transfers between devices, per_device(): lax.all_to_all(spectrum, 'row', split_axis=3, concat_axis=2, tiled=True)  85.5 us
    all_gather x1, waiting for transfers between devices, per_device(): misfit_block = lax.all_gather(misfit, 'depth', axis=0, tiled=True)  43 us
    unnamed x3, waiting for transfers between devices  39.3 us
  transfers between devices with their start and end apart: 7, of which 6 were waited for; matrix products, arithmetic and copies ran while one was open for 3% of the time, Pallas kernels for 0%

commit v1 on v0

--- a/solution.py
+++ b/solution.py
@@ -174,7 +174,12 @@
     image_part = transform_last(by_rows, inverse_tables, False, True)
     image_sum = lax.psum_scatter(image_part, "depth", scatter_dimension=0, tiled=True)
     misfit = image_sum - hologram_part
-    misfit_block = lax.all_gather(misfit, "depth", axis=0, tiled=True)
+    misfit_block = jnp.concatenate(
+        jax.lax.all_to_all(
+            jnp.stack([misfit for _ in range(jax.lax.axis_size("depth"))]), "depth", 0, 0
+        ),
+        axis=0,
+    )
     misfit_pair = transform_last(misfit_block, forward_tables, True, False)
     misfit_spec = lax.all_to_all(misfit_pair, "row", split_axis=2, concat_axis=1, tiled=True)
     misfit_spec = transform_rows(misfit_spec, forward_tables)

time: 1060 us -> 1060 us (level)
  waiting for transfers between devices: 322 us -> 279 us
  blocking collectives: 314 us -> 340 us
    all_gather x1 -> x0, waiting for transfers between devices: 43 us -> none  [per_device(): misfit_block = lax.all_gather(misfit, 'depth', axis=0, tiled=True)]
    all_to_all x0 -> x1, blocking collectives: none -> 24.9 us  [per_device(): jax.lax.all_to_all(jnp.stack([misfit for _ in range(jax.lax.axis_size('de...]
    unnamed x3 -> x2, waiting for transfers between devices: 39.3 us -> 39.9 us
  transfers between devices with their start and end apart: 7 -> 6, of which waited for: 6 -> 5; matrix products, arithmetic and copies ran while one was open for 3% -> 3% of each run, Pallas kernels for 0% -> 0%
where the time goes in v1:
time: 1060 us; the launch traced here: 1050 us
  blocking collectives  340 us (32%)
  waiting for transfers between devices  279 us (26%)
  local copies, waits for them, and re-layouts  171 us (16%)
  matrix products  138 us (13%)
  other arithmetic  81.3 us (8%)
  starting transfers between devices  21.1 us (2%)
  between operations  15 us (1%)
    ppermute x4, waiting for transfers between devices, passed_along(): return lax.ppermute(block, axis, route)  154 us
    dot_general x16, matrix products, contract(): jnp.einsum(formula, table, data, precision=lax.Precision.HIGHEST, preferr...  138 us
    all_to_all x1, blocking collectives, per_device(): lax.all_to_all(misfit_pair, 'row', split_axis=2, concat_axis=1, tiled=True)  108 us
    all_to_all x1, blocking collectives, per_device(): lax.all_to_all(summed, 'row', split_axis=1, concat_axis=2, tiled=True)  106 us
    all_to_all x1, blocking collectives, per_device(): lax.all_to_all(adjoint, 'row', split_axis=2, concat_axis=3, tiled=True)  101 us
    all_to_all x1, waiting for transfers between devices, per_device(): lax.all_to_all(spectrum, 'row', split_axis=3, concat_axis=2, tiled=True)  85.5 us
    unnamed x2, waiting for transfers between devices  39.9 us
    reshape x2, local copies, waits for them, and re-layouts, transform_last(): result.reshape((result.shape[0],) + leading + (outer_len * inner_len,))  31.9 us
  transfers between devices with their start and end apart: 6, of which 5 were waited for; matrix products, arithmetic and copies ran while one was open for 3% of the time, Pallas kernels for 0%

profile of v1, /device:TPU:34, one launch (start us, length us, event | category | flops | bytes accessed | tf_op | source)
XLA Modules:
  0.0 1045.2 jit_solution(5366026882660989310)
XLA Ops:
  12.7 17.3 %fusion.101 = (f32[1,64,64,64]{2,3,0,1:T(8,128)S(1)}, f32[1,64,64,64]{2,3,0,1:T(8,128)}, f32[1,64,64,64]{2,3,0,1:T(8,128)}, f32[1,64,64,64]{2,3,0,1:T(8,128)}, f...) fusion(s32[64,64]{0,1:T(8,128)S(1)} %broadcast_multiply_fusion.3, s32[64,64]{1,0:T(8,128)S(1)} %copy.91), kind=kLoop, calls=%fused_computation.103 | loop fusion | flops 4980736 | bytes 6324224 | tf_op jit(solution)/shard_map/neg | solution.py:28
  38.1 11.0 %fusion.51 = f32[2,1,128,64,64]{2,3,0,4,1:T(8,128)S(1)} fusion(f32[1,2,64,64,64]{3,4,1,0,2:T(8,128)S(1)} %get-tuple-element.13, f32[1,2,64,64,64]{3,4,1,0,2:T(8,128)S(1)} %get-tuple-element.12, f32[2,128,64,64,1]{1,2,3,0,4:T(8,128)S(1)} %fusion.48), kind=kOutput, calls=%fused_computation.67 | convolution fusion | flops 1611661312 | bytes 12582912 | tf_op jit(solution)/shard_map/rqkbm,q...kb->r...mk/dot_general | solution.py:49
  51.6 16.2 %copy.95 = f32[2,1,128,4096]{2,0,1,3:T(2,128)} copy(f32[2,1,128,4096]{2,3,0,1:T(8,128)S(1)} %bitcast.249) | data formatting | bytes 8388608 | tf_op jit(solution)/shard_map/reshape | solution.py:65
  67.8 10.3 all-to-all-start
  79.2 8.6 fusion.43
  87.8 85.5 %all-to-all-done = f32[2,1,128,4096]{2,0,1,3:T(2,128)} async-done(((f32[2,1,128,4096]{2,0,1,3:T(2,128)}), f32[2,1,128,4096]{2,0,1,3:T(2,128)}, u32[]{:S(2)}, u32[]{:S(2)}) %all-to-all-start) | async-done | bytes 4194336 | tf_op jit(solution)/shard_map/all_to_all | solution.py:168
  183.5 8.8 fusion.54
  192.3 10.0 fusion.57
  202.3 8.3 multiply_add_fusion.1
  214.5 10.4 fusion.78
  227.3 15.6 %copy.105 = f32[2,4096,128]{2,0,1:T(2,128)S(1)} copy(f32[2,4096,128]{2,1,0:T(8,128)S(1)} %bitcast.252) | data formatting | bytes 8388608 | tf_op jit(solution)/shard_map/reshape | solution.py:78
  243.0 105.9 %all_to_all.65 = f32[2,4096,128]{2,0,1:T(2,128)S(1)} all-to-all(f32[2,4096,128]{2,0,1:T(2,128)S(1)} %copy.105), channel_id=1, replica_groups=mesh['depth'=8,'row'=32] {'row'}, dimensions={1} | all-to-all | bytes 8388608 | tf_op jit(solution)/shard_map/all_to_all | solution.py:173
  356.8 8.8 fusion.63
  378.3 39.8 %reduce-scatter.4.cloned.1.call-done = f32[16,4096]{1,0:T(8,128)} async-done(((f32[128,4096]{1,0:T(8,128)}), f32[16,4096]{1,0:T(8,128)}) %reduce-scatter.4.cloned.1.call-update) | async-done | bytes 262160
  426.5 24.9 %all_to_all.66 = f32[8,16,4096]{2,1,0:T(8,128)S(1)} all-to-all(f32[8,16,4096]{2,1,0:T(8,128)S(1)} %stack.118), channel_id=1, replica_groups=mesh['depth'=8,'row'=32] {'depth'}, dimensions={0} | all-to-all | bytes 4194304 | tf_op jit(solution)/shard_map/all_to_all | solution.py:178
  454.5 10.5 %fusion.44 = f32[2,128,64,64,1]{2,3,0,1,4:T(8,128)} fusion(f32[128,64,64]{2,1,0:T(8,128)} %reshape.609, f32[1,2,64,64]{3,2,1,0:T(8,128)S(1)} %get-tuple-element.24, f32[1,2,64,64]{3,2,1,0:T(8,128)S(1)} %get-tuple-element.25), kind=kOutput, calls=%fused_computation.62 | convolution fusion | flops 805314560 | bytes 6356992 | tf_op jit(solution)/shard_map/rqka,q...ab->r...kb/dot_general | solution.py:49
  465.0 8.8 copy.155
  473.8 10.6 %fusion.47 = f32[2,128,64,64]{1,2,0,3:T(8,128)S(1)} fusion(f32[2,128,64,64,1]{1,3,0,4,2:T(8,128)} %copy.155, f32[1,2,64,64,64]{3,4,1,0,2:T(8,128)} %copy-done.5, f32[1,2,64,64,64]{3,4,1,0,2:T(8,128)} %copy-done.2), kind=kOutput, calls=%fused_computation.65 | convolution fusion | flops 1611661312 | bytes 12582912 | tf_op jit(solution)/shard_map/rqkbm,q...kb->r...mk/dot_general | solution.py:49
  486.9 15.6 %copy.116 = f32[2,128,4096]{1,0,2:T(2,128)S(1)} copy(f32[2,128,4096]{1,2,0:T(8,128)S(1)} %bitcast.255) | data formatting | bytes 8388608 | tf_op jit(solution)/shard_map/reshape | solution.py:65
  502.5 107.6 %all_to_all.67 = f32[2,128,4096]{1,0,2:T(2,128)S(1)} all-to-all(f32[2,128,4096]{1,0,2:T(2,128)S(1)} %copy.116), channel_id=1, replica_groups=mesh['depth'=8,'row'=32] {'row'}, dimensions={2} | all-to-all | bytes 8388608 | tf_op jit(solution)/shard_map/all_to_all | solution.py:184
  618.1 8.7 fusion.66
  626.8 10.0 fusion.69
  636.8 8.3 multiply_subtract_fusion
  649.2 10.4 fusion.83
  662.0 15.6 %copy.126 = f32[2,1,4096,128]{3,0,1,2:T(2,128)S(1)} copy(f32[2,1,4096,128]{3,2,0,1:T(8,128)S(1)} %bitcast.257) | data formatting | bytes 8388608 | tf_op jit(solution)/shard_map/reshape | solution.py:78
  677.6 101.2 %all_to_all.68 = f32[2,1,4096,128]{3,0,1,2:T(2,128)S(1)} all-to-all(f32[2,1,4096,128]{3,0,1,2:T(2,128)S(1)} %copy.126), channel_id=1, replica_groups=mesh['depth'=8,'row'=32] {'row'}, dimensions={2} | all-to-all | bytes 8388608 | tf_op jit(solution)/shard_map/all_to_all | solution.py:189
  786.7 8.8 fusion.75
  795.6 10.0 fusion.13
  832.8 71.7 %collective-permute-done = f32[2,1,128,4096]{2,3,0,1:T(8,128)} collective-permute-done((f32[2,1,128,4096]{2,3,0,1:T(8,128)}, f32[2,1,128,4096]{2,3,0,1:T(8,128)}, u32[]{:S(2)}, u32[]{:S(2)}) %collective-permute-start) | collective-permute-done | bytes 4194336 | tf_op jit(solution)/shard_map/ppermute | solution.py:14
  904.4 9.1 add_reduce_fusion
  939.5 78.9 %collective-permute-done.2 = f32[2,1,128,4096]{2,3,0,1:T(8,128)} collective-permute-done((f32[2,1,128,4096]{2,3,0,1:T(8,128)}, f32[2,1,128,4096]{2,3,0,1:T(8,128)}, u32[]{:S(2)}, u32[]{:S(2)}) %collective-permute-start.2) | collective-permute-done | bytes 4194336 | tf_op jit(solution)/shard_map/ppermute | solution.py:14
  1018.4 13.9 %fusion.10 = f32[2,1,128,4096]{2,3,0,1:T(8,128)} fusion(f32[2,1,128,4096]{2,3,0,1:T(8,128)} %bitcast_subtract_fusion, f32[2,1,128,4096]{2,3,0,1:T(8,128)} %copy-done.8, f32[2,1,127,4096]{2,3,0,1:T(8,128)} %bitcast.244, f32[2,1,1,4096]{2,3,0,1:T(8,128)} %copy.137, f32[2,1,128,4096]{2,3,0,1:T(8,128)} %get-tuple-element.7, f32[2,1,128,4095]{2,3,0,1:T(8,128)} %bitcast.245, ...), kind=kLoop, calls=%fused_computation.21 | loop fusion | flops 8388608 | bytes 33553408 | tf_op jit(solution)/shard_map/add | solution.py:146
  (104 shorter events, 148.9 us)
Async XLA Ops:
  6.5 371.1 %copy-start = (f32[128,4096]{1,0:T(8,128)S(1)}, f32[128,4096]{1,0:T(8,128)}, u32[]{:S(2)}) copy-start(f32[128,4096]{1,0:T(8,128)} %param.4) | copy-start | bytes 6291460
  30.0 2.2 copy-start.15
  31.7 6.4 copy-start.2
  31.7 6.4 copy-start.5
  67.8 105.6 %all-to-all-start = ((f32[2,1,128,4096]{2,0,1,3:T(2,128)}), f32[2,1,128,4096]{2,0,1,3:T(2,128)}, u32[]{:S(2)}, u32[]{:S(2)}) async-start(f32[2,1,128,4096]{2,0,1,3:T(2,128)} %copy.95), calls=%async_computation | async-start | bytes 8388608 | tf_op jit(solution)/shard_map/all_to_all | solution.py:168
  78.1 340.0 %reduce-scatter.4.cloned.1.call-start = ((), (), s32[]{:S(2)}) async-start(), calls=%async_computation.6 | async-start | bytes 2359296
  183.5 8.8 copy-start.3
  183.5 8.8 copy-start.6
  210.6 3.9 copy-start.9
  210.6 3.9 copy-start.12
  356.8 8.8 copy-start.20
  356.8 8.8 copy-start.21
  618.1 8.7 copy-start.4
  618.1 8.7 copy-start.7
  645.1 4.1 copy-start.10
  645.1 4.1 copy-start.13
  786.7 8.8 copy-start.11
  786.7 8.8 copy-start.14
  805.6 2.7 copy-start.16
  810.6 93.8 %collective-permute-start = (f32[2,1,128,4096]{2,3,0,1:T(8,128)}, f32[2,1,128,4096]{2,3,0,1:T(8,128)}, u32[]{:S(2)}, u32[]{:S(2)}) collective-permute-start(f32[2,1,128,4096]{2,3,0,1:T(8,128)} %bitcast_subtract_fusion), channel_id=1, source_target_pairs={{32,0},{64,32},{96,64},{128,96},{160,128},{192,160},{224,192},{33,... | collective-permute-start | bytes 12582920 | tf_op jit(solution)/shard_map/ppermute | solution.py:14
  817.6 12.5 %collective-permute-start.1 = (f32[2,1,1,4096]{3,0,2,1:T(2,128)S(1)}, f32[2,1,1,4096]{3,0,2,1:T(2,128)S(1)}, u32[]{:S(2)}, u32[]{:S(2)}) collective-permute-start(f32[2,1,1,4096]{3,0,2,1:T(2,128)S(1)} %copy.134), channel_id=1, source_target_pairs={{1,0},{2,1},{3,2},{4,3},{5,4},{6,5},{7,6},{8,7},{9,8},{10,9},{11,1... | collective-permute-start | bytes 98312 | tf_op jit(solution)/shard_map/ppermute | solution.py:14
  904.4 9.9 copy-start.18
  904.4 9.9 copy-start.19
  913.5 2.3 copy-start.17
  923.0 2.7 copy-start.8
  923.0 95.5 %collective-permute-start.2 = (f32[2,1,128,4096]{2,3,0,1:T(8,128)}, f32[2,1,128,4096]{2,3,0,1:T(8,128)}, u32[]{:S(2)}, u32[]{:S(2)}) collective-permute-start(f32[2,1,128,4096]{2,3,0,1:T(8,128)} %get-tuple-element.5), channel_id=1, source_target_pairs={{0,32},{32,64},{64,96},{96,128},{128,160},{160,192},{192,224},{1,3... | collective-permute-start | bytes 12582920 | tf_op jit(solution)/shard_map/ppermute | solution.py:14
  931.7 5.2 collective-permute-start.3
  1018.4 19.5 %copy-start.1 = (f32[128,4096]{1,0:T(8,128)S(1)}, f32[128,4096]{1,0:T(8,128)}, u32[]{:S(2)}) copy-start(f32[128,4096]{1,0:T(8,128)} %param.4) | copy-start | bytes 6291460
Sparse Core Ops, SparseCore 0:
  377.7 40.3 reduce-scatter.3
